TPU v7x, 32 devices: a whole 2x2x4 slice. The times are simulated.
32 devices in a mesh: prow: 4 (over y, core), pcol: 8 (over z, x).
Axes of the slice: x: 2, y: 2, z: 4, core: 2. Of those that a mesh axis runs over, the one named last changes fastest.
Arguments:
- matrix: bfloat16 [4096, 2048], P('prow', 'pcol'), may hold values from -6 to 6
- panel_one: bfloat16 [256, 4096], P('pcol', 'prow'), may hold values from -0.375 to 0.375
- panel_two: bfloat16 [256, 4096], P('pcol', 'prow'), may hold values from -0.375 to 0.375
- pivots_one: int32 [256], replicated, may hold values from 0 to 4095, as said below
- pivots_two: int32 [256], replicated, may hold values from 256 to 4095, as said below
Outputs:
- trailing: bfloat16 [4096, 2048], P('prow', 'pcol')
Inputs may be any that keep to these rules, and one draw needn't show every extreme that they name: Each pivots_one[i] is either i or a logical row from 256 to 4095; no row is named twice; 4095 is always named. Each pivots_two[i] is either 256 + i or a logical row from 512 to 4095; no row is named twice; 4095 is always named.
All inputs are finite; a program needn't handle non-finite values.
Results may differ from a plain program's by a relative error of at most 0.006.
Values may be sent and summed in bfloat16 or wider, within the bound.
A program may use at most 64 MiB of HBM per device.

v0:
```python
import jax
import jax.numpy as jnp
from jax import lax
from jax.sharding import PartitionSpec as P


def spread(block, axis, source):
    block = jnp.where(lax.axis_index(axis) == source, block, jnp.zeros_like(block))
    return lax.psum(block, axis)


def logical_rows(local_rows, row_index, process_rows, width):
    return (local_rows // width * process_rows + row_index) * width + local_rows % width


def stored_place(logical, process_rows, width):
    owner_row = logical // width % process_rows
    local_row = logical // width // process_rows * width + logical % width
    return (owner_row, local_row)


def trade_order(pivots, first_row, total_rows):
    width = pivots.shape[0]
    order_map = jnp.arange(total_rows, dtype=jnp.int32)
    pivot_at = first_row + jnp.arange(width, dtype=jnp.int32)
    order_map = order_map.at[pivots].set(pivot_at)
    return order_map.at[pivot_at].set(pivots)


def swap_local(current, old_block, order_map, logical, first_row, width):
    source = jnp.take(order_map, logical)
    is_moved = (logical >= first_row + width) & (source != logical)
    filled = jnp.take(old_block, jnp.clip(source - first_row, 0, width - 1), axis=0)
    return jnp.where(is_moved[:, None], filled, current)


def unit_inverse(strict):
    extent = strict.shape[0]
    identity = jnp.eye(extent, dtype=jnp.float32)
    result = identity - strict
    powered = strict
    for repeat in range((extent - 1).bit_length() - 1):
        powered = jnp.dot(powered, powered, precision=lax.Precision.HIGHEST)
        result = jnp.dot(result, identity + powered, precision=lax.Precision.HIGHEST)
    return result


def pivot_solve(incoming, diagonal, section_index, process_rows):
    strict = jnp.tril(diagonal.T.astype(jnp.float32), -1)
    solved = jnp.dot(
        unit_inverse(strict), incoming.astype(jnp.float32), precision=lax.Precision.HIGHEST
    ).astype(jnp.bfloat16)
    solved = spread(solved, "prow", section_index % process_rows)
    return solved


def collect(picker, order_map, first_row, section_index, row_index, process_rows, width):
    sources = order_map[first_row : first_row + width]
    owner_row, local_row = stored_place(sources, process_rows, width)
    is_mine = (owner_row == row_index).astype(jnp.float32)[:, None]
    arriving = picker(local_row).astype(jnp.float32) * is_mine
    block_local = section_index // process_rows * width + jnp.arange(width, dtype=jnp.int32)
    holder = (row_index == section_index % process_rows).astype(jnp.float32)
    leaving = picker(block_local).astype(jnp.float32) * holder
    summed = lax.psum(
        jnp.concatenate([arriving, leaving], axis=0).astype(jnp.bfloat16), "prow"
    ).astype(jnp.float32)
    incoming = summed[:width].astype(jnp.bfloat16)
    old_block = summed[width:].astype(jnp.bfloat16)
    return (incoming, old_block)


def finish(swapped, solved, panel_all, logical, first_row, width):
    product = lax.dot_general(
        panel_all, solved, (((0,), (0,)), ((), ())), preferred_element_type=jnp.float32
    )
    updated = (swapped.astype(jnp.float32) - product).astype(jnp.bfloat16)
    pivot_part = jnp.take(solved, jnp.clip(logical - first_row, 0, width - 1), axis=0)
    in_block = (logical >= first_row) & (logical < first_row + width)
    beyond = logical >= first_row + width
    return jnp.where(beyond[:, None], updated, jnp.where(in_block[:, None], pivot_part, swapped))


def on_device(matrix, panel_one, panel_two, pivots_one, pivots_two):
    rows_dev = matrix.shape[0]
    process_rows = lax.axis_size("prow")
    row_index = lax.axis_index("prow")
    width = panel_one.shape[0] * lax.axis_size("pcol")
    total_rows = rows_dev * process_rows
    logical = logical_rows(jnp.arange(rows_dev, dtype=jnp.int32), row_index, process_rows, width)
    start_two = 1 // process_rows * width
    panel_all_one, panel_all_two = (
        lax.all_gather(panel_one, "pcol", axis=0, tiled=True),
        lax.all_gather(panel_two, "pcol", axis=0, tiled=True),
    )
    diagonal_one = panel_all_one[:, 0:width]
    diagonal_two = panel_all_two[:, start_two : start_two + width]
    order_one = trade_order(pivots_one, 0, total_rows)
    order_two = trade_order(pivots_two, width, total_rows)
    incoming_one, old_one = collect(
        lambda local_row: jnp.take(matrix, local_row, axis=0),
        order_one,
        0,
        0,
        row_index,
        process_rows,
        width,
    )
    swapped_one = swap_local(matrix, old_one, order_one, logical, 0, width)
    solved_one = pivot_solve(incoming_one, diagonal_one, 0, process_rows)
    after_one = finish(swapped_one, solved_one, panel_all_one, logical, 0, width)
    incoming_two, old_two = collect(
        lambda local_row: jnp.take(after_one, local_row, axis=0),
        order_two,
        width,
        1,
        row_index,
        process_rows,
        width,
    )
    swapped_two = swap_local(after_one, old_two, order_two, logical, width, width)
    solved_two = pivot_solve(incoming_two, diagonal_two, 1, process_rows)
    return finish(swapped_two, solved_two, panel_all_two, logical, width, width)


def solution(mesh):
    placed = (P("prow", "pcol"), P("pcol", "prow"), P("pcol", "prow"), P(), P())
    return jax.shard_map(
        on_device, mesh=mesh, in_specs=placed, out_specs=P("prow", "pcol"), check_vma=False
    )
```

profile of v0, /device:TPU:0, one launch (start us, length us, event | category | flops | bytes accessed | tf_op | source)
XLA Modules:
  0.0 230.9 jit_solution(7140232656776959476)
XLA Ops:
  6.5 0.7 copy-done.5
  7.2 1.4 scatter_fusion.2
  8.7 1.4 scatter_fusion.3
  10.3 1.2 gather_fusion.2
  11.4 1.2 gather_fusion.3
  12.7 0.7 pad_maximum_fusion
  13.5 0.8 copy-done.3
  14.3 33.0 %all_gather.6 = bf16[256,1024]{1,0:T(8,128)(2,1)S(1)} all-gather(bf16[32,1024]{1,0:T(8,128)(2,1)S(1)} %copy-done.3), channel_id=1, replica_groups=mesh['prow'=4,'pcol'=8] {'pcol'}, dimensions={0}, use_global_device_ids=true | all-gather | bytes 589824 | tf_op jit(solution)/shard_map/all_gather | solution.py:93
  47.4 0.5 fusion.21
  47.9 0.4 fusion.8
  48.7 6.2 %gather_fusion.1 = s32[1024]{0:T(1024)S(1)} fusion(s32[4096]{0:T(1024)S(1)} %scatter_fusion.3, s32[1024]{0:T(1024)S(1)} %fusion.43), kind=kCustom, calls=%fused_computation.3.clone | custom fusion | bytes 12288 | tf_op jit(solution)/shard_map/jit(_take)/gather | solution.py:31
  55.0 0.7 copy-done.6
  55.7 1.4 scatter_fusion
  57.1 1.4 scatter_fusion.1
  58.6 6.2 %gather_fusion = s32[1024]{0:T(1024)S(1)} fusion(s32[4096]{0:T(1024)S(1)} %scatter_fusion.1, s32[1024]{0:T(1024)S(1)} %fusion.43), kind=kCustom, calls=%fused_computation.clone | custom fusion | bytes 12288 | tf_op jit(solution)/shard_map/jit(_take)/gather | solution.py:31
  64.8 31.5 %all_gather.7 = bf16[256,1024]{1,0:T(8,128)(2,1)S(1)} all-gather(bf16[32,1024]{1,0:T(8,128)(2,1)S(1)} %copy-done.4), channel_id=1, replica_groups=mesh['prow'=4,'pcol'=8] {'pcol'}, dimensions={0}, use_global_device_ids=true | all-gather | bytes 589824 | tf_op jit(solution)/shard_map/all_gather | solution.py:94
  96.4 0.5 fusion.20
  96.8 0.4 fusion.14
  97.3 0.4 fusion.60
  98.1 0.4 fusion.9
  98.8 0.4 fusion.10
  99.6 0.4 fusion.11
  100.4 0.4 fusion.12
  101.2 0.4 fusion.13
  102.1 0.4 fusion.15
  102.9 0.4 fusion.16
  103.6 0.4 fusion.17
  104.4 0.4 fusion.18
  105.2 0.4 fusion.19
  106.7 1.8 fusion.6
  108.9 0.9 slice-done
  109.8 3.9 %gather_fusion.4 = bf16[1024,256]{1,0:T(8,128)(2,1)S(1)} fusion(bf16[256,256]{1,0:T(8,128)(2,1)S(1)} %slice-done, s32[1024]{0:T(1024)S(1)} %get-tuple-element.23), kind=kCustom, calls=%fused_computation.2.clone | custom fusion | bytes 1052672 | tf_op jit(solution)/shard_map/jit(_take)/gather | solution.py:33
  113.7 1.0 copy.26
  114.7 26.7 %all-reduce.7.cloned.1.call-done = bf16[256,256]{1,0:T(8,128)(2,1)} async-done(((bf16[256,256]{1,0:T(8,128)(2,1)}), bf16[256,256]{1,0:T(8,128)(2,1)}) %all-reduce.7.cloned.1.call-update) | async-done | bytes 131088 | tf_op jit(solution)/shard_map/psum | solution.py:9
  141.4 4.4 %gather_fusion.5 = bf16[1024,256]{1,0:T(8,128)(2,1)S(1)} fusion(bf16[256,256]{1,0:T(8,128)(2,1)} %all-reduce.7.cloned.1.call-done, s32[1024]{0:T(1024)S(1)} %get-tuple-element.22), kind=kCustom, calls=%fused_computation.7.clone | custom fusion | bytes 1052672 | tf_op jit(solution)/shard_map/jit(_take)/gather | solution.py:78
  145.8 1.0 copy.29
  146.8 1.5 fusion.5
  148.5 1.2 gather_fusion.7
  149.7 1.2 gather_fusion.6
  151.1 0.7 pad_maximum_fusion.1
  151.9 32.0 %all-reduce.9.cloned.1.call-done = bf16[512,256]{1,0:T(8,128)(2,1)} async-done(((bf16[512,256]{1,0:T(8,128)(2,1)}), bf16[512,256]{1,0:T(8,128)(2,1)}) %all-reduce.9.cloned.1.call-update) | async-done | bytes 262160 | tf_op jit(solution)/shard_map/psum | solution.py:65
  184.0 1.8 fusion.7
  185.9 0.9 slice-done.1
  186.8 3.9 %gather_fusion.8 = bf16[1024,256]{1,0:T(8,128)(2,1)S(1)} fusion(bf16[256,256]{1,0:T(8,128)(2,1)S(1)} %slice-done.1, s32[1024]{0:T(1024)S(1)} %get-tuple-element.25), kind=kCustom, calls=%fused_computation.8.clone | custom fusion | bytes 1052672 | tf_op jit(solution)/shard_map/jit(_take)/gather | solution.py:33
  190.9 26.8 %all-reduce.11.cloned.1.call-done = bf16[256,256]{1,0:T(8,128)(2,1)} async-done(((bf16[256,256]{1,0:T(8,128)(2,1)}), bf16[256,256]{1,0:T(8,128)(2,1)}) %all-reduce.11.cloned.1.call-update) | async-done | bytes 131088 | tf_op jit(solution)/shard_map/psum | solution.py:9
  217.7 4.4 %gather_fusion.9 = bf16[1024,256]{1,0:T(8,128)(2,1)S(1)} fusion(bf16[256,256]{1,0:T(8,128)(2,1)} %all-reduce.11.cloned.1.call-done, s32[1024]{0:T(1024)S(1)} %get-tuple-element.24), kind=kCustom, calls=%fused_computation.9.clone | custom fusion | bytes 1052672 | tf_op jit(solution)/shard_map/jit(_take)/gather | solution.py:78
  222.3 0.7 copy-done.1
  223.3 1.0 copy.35
  (73 shorter events, 7.5 us)
Async XLA Ops:
  6.5 100.2 %all-reduce.5.cloned.1.call-start = ((), (), s32[]{:S(2)}) async-start(), calls=%async_computation | async-start | bytes 524288 | tf_op jit(solution)/shard_map/psum | solution.py:65
  6.5 0.7 copy-start.5
  8.7 1.6 copy-start.2
  13.5 0.8 copy-start.3
  13.5 127.9 %all-reduce.7.cloned.1.call-start = ((), (), s32[]{:S(2)}) async-start(), calls=%async_computation.1 | async-start | bytes 262144 | tf_op jit(solution)/shard_map/psum | solution.py:9
  55.0 0.7 copy-start.6
  58.6 6.2 %copy-start.4 = (bf16[32,1024]{1,0:T(8,128)(2,1)S(1)}, bf16[32,1024]{1,0:T(8,128)(2,1)}, u32[]{:S(2)}) copy-start(bf16[32,1024]{1,0:T(8,128)(2,1)} %param.13) | copy-start | bytes 196612
  108.6 75.4 %all-reduce.9.cloned.1.call-start = ((), (), s32[]{:S(2)}) async-start(), calls=%async_computation.2 | async-start | bytes 524288 | tf_op jit(solution)/shard_map/psum | solution.py:65
  108.8 0.9 slice-start
  145.8 1.0 copy-start
  151.8 65.8 %all-reduce.11.cloned.1.call-start = ((), (), s32[]{:S(2)}) async-start(), calls=%async_computation.3 | async-start | bytes 262144 | tf_op jit(solution)/shard_map/psum | solution.py:9
  185.9 0.9 slice-start.1
  222.1 0.9 copy-start.1
Sparse Core Ops, SparseCore 0:
  13.6 34.6 all-reduce.4
  108.7 32.6 all-reduce.6
  152.0 31.9 all-reduce.8
  186.3 31.3 all-reduce.10
where the time goes:
time: 231 us
  waiting for transfers between devices  85.6 us (37%)
  blocking collectives  64.5 us (28%)
  local copies, waits for them, and re-layouts  48 us (21%)
  matrix products  16.7 us (7%)
  between operations  13.7 us (6%)
    psum x2, waiting for transfers between devices, spread(): return lax.psum(block, axis)  53.4 us
    all_gather x1, blocking collectives, on_device(): lax.all_gather(panel_one, 'pcol', axis=0, tiled=True)  33 us
    psum x2, waiting for transfers between devices, collect(): lax.psum(jnp.concatenate([arriving, leaving], axis=0).astype(jnp.bfloat16...  32.1 us
    all_gather x1, blocking collectives, on_device(): lax.all_gather(panel_two, 'pcol', axis=0, tiled=True)  31.5 us
    gather x2, local copies, waits for them, and re-layouts, swap_local(): source = jnp.take(order_map, logical)  12.3 us
    gather x4, local copies, waits for them, and re-layouts, finish(): jnp.take(solved, jnp.clip(logical - first_row, 0, width - 1), axis=0)  9.97 us
    gather x4, local copies, waits for them, and re-layouts, swap_local(): jnp.take(old_block, jnp.clip(source - first_row, 0, width - 1), axis=0)  9.09 us
    dot_general x14, matrix products, unit_inverse(): jnp.dot(result, identity + powered, precision=lax.Precision.HIGHEST)  5.62 us
  transfers between devices with their start and end apart: 4, of which 3 were waited for; matrix products, arithmetic and copies ran while one was open for 16% of the time, Pallas kernels for 0%

commit v1 on v0

--- a/solution.py
+++ b/solution.py
@@ -2,6 +2,28 @@
 import jax.numpy as jnp
 from jax import lax
 from jax.sharding import PartitionSpec as P
+
+
+def joined_along(blocks, dim):
+    blocks = jnp.moveaxis(blocks, 0, dim)
+    lengths = blocks.shape
+    return blocks.reshape(*lengths[:dim], lengths[dim] * lengths[dim + 1], *lengths[dim + 2 :])
+
+
+def ring_gather(x, axis, dim):
+    size = lax.axis_size(axis)
+    pairs = [(i, (i + 1) % size) for i in range(size)]
+    back = [(b, a) for a, b in pairs]
+    lower, upper = ([], [])
+    for turn in range(size - 1):
+        if turn % 2 == 0:
+            lower.append(lax.ppermute(lower[-1] if lower else x, axis, pairs))
+        else:
+            upper.append(lax.ppermute(upper[-1] if upper else x, axis, back))
+    blocks = jnp.stack([*lower[::-1], x, *upper])
+    shift = lax.axis_index(axis) - len(lower)
+    blocks = blocks[(jnp.arange(size) - shift) % size]
+    return joined_along(blocks, dim)
 
 
 def spread(block, axis, source):
@@ -91,7 +113,7 @@
     start_two = 1 // process_rows * width
     panel_all_one, panel_all_two = (
         lax.all_gather(panel_one, "pcol", axis=0, tiled=True),
-        lax.all_gather(panel_two, "pcol", axis=0, tiled=True),
+        ring_gather(panel_two, "pcol", 0),
     )
     diagonal_one = panel_all_one[:, 0:width]
     diagonal_two = panel_all_two[:, start_two : start_two + width]

time: 231 us -> 206 us (0.89)
  blocking collectives: 64.5 us -> 31.3 us
  waiting for transfers between devices: 85.6 us -> 66.9 us
  starting transfers between devices: 0.35 us -> 17.3 us
  other arithmetic: 2.1 us -> 7.82 us
  local copies, waits for them, and re-layouts: 48 us -> 52.5 us
    all_gather x1 -> x0, blocking collectives: 31.5 us -> none  [on_device(): lax.all_gather(panel_two, 'pcol', axis=0, tiled=True)]
    ppermute x0 -> x7, starting transfers between devices: none -> 17 us  [the longest x3 12.5 us: ring_gather(): upper.append(lax.ppermute(upper[-1] if upper else x, axis, back))]
    psum x2, waiting for transfers between devices: 32.1 us -> 16.8 us  [collect(): lax.psum(jnp.concatenate([arriving, leaving], axis=0).astype(jnp.bfloat16...]
    psum x2, waiting for transfers between devices: 53.4 us -> 45.6 us  [spread(): return lax.psum(block, axis)]
    unnamed x17 -> x58, local copies, waits for them, and re-layouts: 3.2 us -> 8.18 us
    ppermute x0 -> x7, waiting for transfers between devices: none -> 4.49 us  [the longest x4 4.49 us: ring_gather(): lower.append(lax.ppermute(lower[-1] if lower else x, axis, pairs))]
  transfers between devices with their start and end apart: 4 -> 11, of which waited for: 3 -> 4; matrix products, arithmetic and copies ran while one was open for 16% -> 30% of each run, Pallas kernels for 0% -> 0%
where the time goes in v1:
time: 206 us
  waiting for transfers between devices  66.9 us (32%)
  local copies, waits for them, and re-layouts  52.5 us (25%)
  blocking collectives  31.3 us (15%)
  starting transfers between devices  17.3 us (8%)
  matrix products  16.2 us (8%)
  between operations  13.9 us (7%)
  other arithmetic  7.82 us (4%)
    psum x2, waiting for transfers between devices, spread(): return lax.psum(block, axis)  45.6 us
    all_gather x1, blocking collectives, on_device(): lax.all_gather(panel_one, 'pcol', axis=0, tiled=True)  31.3 us
    psum x2, waiting for transfers between devices, collect(): lax.psum(jnp.concatenate([arriving, leaving], axis=0).astype(jnp.bfloat16...  16.8 us
    ppermute x3, starting transfers between devices, ring_gather(): upper.append(lax.ppermute(upper[-1] if upper else x, axis, back))  12.5 us
    gather x2, local copies, waits for them, and re-layouts, swap_local(): source = jnp.take(order_map, logical)  12.3 us
    gather x4, local copies, waits for them, and re-layouts, finish(): jnp.take(solved, jnp.clip(logical - first_row, 0, width - 1), axis=0)  9.17 us
    gather x4, local copies, waits for them, and re-layouts, swap_local(): jnp.take(old_block, jnp.clip(source - first_row, 0, width - 1), axis=0)  8.28 us
    unnamed x58, local copies, waits for them, and re-layouts  8.18 us
  transfers between devices with their start and end apart: 11, of which 4 were waited for; matrix products, arithmetic and copies ran while one was open for 30% of the time, Pallas kernels for 0%

profile of v1, /device:TPU:0, one launch (start us, length us, event | category | flops | bytes accessed | tf_op | source)
XLA Modules:
  0.0 205.9 jit_solution(1467863529351791671)
XLA Ops:
  6.5 2.9 %collective-permute-start = (bf16[32,1024]{1,0:T(8,128)(2,1)}, bf16[32,1024]{1,0:T(8,128)(2,1)S(1)}, u32[]{:S(2)}, u32[]{:S(2)}) collective-permute-start(bf16[32,1024]{1,0:T(8,128)(2,1)} %param.13), channel_id=1, source_target_pairs={{0,1},{1,2},{2,3},{3,4},{4,5},{5,6},{6,7},{7,0},{8,9},{9,10},{10,1... | collective-permute-start | bytes 196616 | tf_op jit(solution)/shard_map/ppermute | solution.py:20
  9.5 3.0 %collective-permute-start.4 = (bf16[32,1024]{1,0:T(8,128)(2,1)}, bf16[32,1024]{1,0:T(8,128)(2,1)S(1)}, u32[]{:S(2)}, u32[]{:S(2)}) collective-permute-start(bf16[32,1024]{1,0:T(8,128)(2,1)} %param.13), channel_id=1, source_target_pairs={{1,0},{2,1},{3,2},{4,3},{5,4},{6,5},{7,6},{0,7},{9,8},{10,9},{11,1... | collective-permute-start | bytes 196616 | tf_op jit(solution)/shard_map/ppermute | solution.py:22
  12.5 0.7 copy-done.10
  13.2 1.4 scatter_fusion.2
  14.7 1.4 scatter_fusion.3
  16.2 1.2 gather_fusion.3
  17.4 1.2 gather_fusion.4
  18.7 0.7 pad_maximum_fusion
  19.6 0.8 copy-done.3
  20.3 31.3 %all_gather.3 = bf16[256,1024]{1,0:T(8,128)(2,1)S(1)} all-gather(bf16[32,1024]{1,0:T(8,128)(2,1)S(1)} %copy-done.3), channel_id=1, replica_groups=mesh['prow'=4,'pcol'=8] {'pcol'}, dimensions={0}, use_global_device_ids=true | all-gather | bytes 589824 | tf_op jit(solution)/shard_map/all_gather | solution.py:115
  53.0 6.2 %gather_fusion.2 = s32[1024]{0:T(1024)S(1)} fusion(s32[4096]{0:T(1024)S(1)} %scatter_fusion.3, s32[1024]{0:T(1024)S(1)} %fusion.42), kind=kCustom, calls=%fused_computation.3.clone | custom fusion | bytes 12288 | tf_op jit(solution)/shard_map/jit(_take)/gather | solution.py:53
  59.2 0.6 compare_and_fusion.7
  59.8 0.7 copy-done.11
  60.5 1.4 scatter_fusion
  61.9 1.6 scatter_fusion.1
  64.1 6.1 %gather_fusion.1 = s32[1024]{0:T(1024)S(1)} fusion(s32[4096]{0:T(1024)S(1)} %scatter_fusion.1, s32[1024]{0:T(1024)S(1)} %fusion.42), kind=kCustom, calls=%fused_computation.clone | custom fusion | bytes 12288 | tf_op jit(solution)/shard_map/jit(_take)/gather | solution.py:53
  70.2 0.6 fusion.44
  75.4 0.6 pad_clamp_fusion.1
  76.6 0.6 pad_clamp_fusion
  77.5 0.6 compare_and_fusion.2
  78.4 0.6 compare_and_fusion
  79.0 4.7 %collective-permute-start.5 = (bf16[32,1024]{1,0:T(8,128)(2,1)S(1)}, bf16[32,1024]{1,0:T(8,128)(2,1)}, u32[]{:S(2)}, u32[]{:S(2)}) collective-permute-start(bf16[32,1024]{1,0:T(8,128)(2,1)S(1)} %collective-permute-done.4), channel_id=1, source_target_pairs={{1,0},{2,1},{3,2},{4,3},{5,4},{6,5},{7,6},{0,7},{9,8},{10,9},{11,1... | collective-permute-start | bytes 196616 | tf_op jit(solution)/shard_map/ppermute | solution.py:22
  83.7 1.8 fusion.5
  86.2 0.9 slice-done
  87.1 3.9 %gather_fusion.5 = bf16[1024,256]{1,0:T(8,128)(2,1)S(1)} fusion(bf16[256,256]{1,0:T(8,128)(2,1)S(1)} %slice-done, s32[1024]{0:T(1024)S(1)} %get-tuple-element.19), kind=kCustom, calls=%fused_computation.2.clone | custom fusion | bytes 1052672 | tf_op jit(solution)/shard_map/jit(_take)/gather | solution.py:55
  91.3 4.7 %collective-permute-start.6 = (bf16[32,1024]{1,0:T(8,128)(2,1)}, bf16[32,1024]{1,0:T(8,128)(2,1)S(1)}, u32[]{:S(2)}, u32[]{:S(2)}) collective-permute-start(bf16[32,1024]{1,0:T(8,128)(2,1)} %collective-permute-done.5), channel_id=1, source_target_pairs={{1,0},{2,1},{3,2},{4,3},{5,4},{6,5},{7,6},{0,7},{9,8},{10,9},{11,1... | collective-permute-start | bytes 196616 | tf_op jit(solution)/shard_map/ppermute | solution.py:22
  96.1 18.8 %all-reduce.7.cloned.1.call-done = bf16[256,256]{1,0:T(8,128)(2,1)} async-done(((bf16[256,256]{1,0:T(8,128)(2,1)}), bf16[256,256]{1,0:T(8,128)(2,1)}) %all-reduce.7.cloned.1.call-update) | async-done | bytes 131088 | tf_op jit(solution)/shard_map/psum | solution.py:31
  114.9 4.4 %gather_fusion.6 = bf16[1024,256]{1,0:T(8,128)(2,1)S(1)} fusion(bf16[256,256]{1,0:T(8,128)(2,1)} %all-reduce.7.cloned.1.call-done, s32[1024]{0:T(1024)S(1)} %get-tuple-element.18), kind=kCustom, calls=%fused_computation.7.clone | custom fusion | bytes 1052672 | tf_op jit(solution)/shard_map/jit(_take)/gather | solution.py:100
  119.5 0.6 copy-done
  120.2 1.0 fusion.4
  121.4 1.3 gather_fusion.8
  122.7 1.3 gather_fusion.7
  124.0 0.6 copy-done.12
  125.4 1.5 collective-permute-start.3
  126.9 0.7 pad_maximum_fusion.1
  128.0 4.5 %collective-permute-done.3 = bf16[32,1024]{1,0:T(8,128)(2,1)S(1)} collective-permute-done((bf16[32,1024]{1,0:T(8,128)(2,1)S(1)}, bf16[32,1024]{1,0:T(8,128)(2,1)S(1)}, u32[]{:S(2)}, u32[]{:S(2)}) %collective-permute-start.3) | collective-permute-done | bytes 65568 | tf_op jit(solution)/shard_map/ppermute | solution.py:20
  132.5 0.8 bitcast_dynamic-update-slice_fusion.5
  133.3 0.8 copy-done.4
  134.2 0.8 bitcast_dynamic-update-slice_fusion.1
  135.0 0.7 gather_fusion
  142.1 16.8 %all-reduce.9.cloned.1.call-done = bf16[512,256]{1,0:T(8,128)(2,1)} async-done(((bf16[512,256]{1,0:T(8,128)(2,1)}), bf16[512,256]{1,0:T(8,128)(2,1)}) %all-reduce.9.cloned.1.call-update) | async-done | bytes 262160 | tf_op jit(solution)/shard_map/psum | solution.py:87
  158.9 1.8 fusion.6
  160.8 0.9 slice-done.1
  161.7 3.9 %gather_fusion.9 = bf16[1024,256]{1,0:T(8,128)(2,1)S(1)} fusion(bf16[256,256]{1,0:T(8,128)(2,1)S(1)} %slice-done.1, s32[1024]{0:T(1024)S(1)} %copy-done.8), kind=kCustom, calls=%fused_computation.8.clone | custom fusion | bytes 1052672 | tf_op jit(solution)/shard_map/jit(_take)/gather | solution.py:55
  165.9 26.7 %all-reduce.11.cloned.1.call-done = bf16[256,256]{1,0:T(8,128)(2,1)} async-done(((bf16[256,256]{1,0:T(8,128)(2,1)}), bf16[256,256]{1,0:T(8,128)(2,1)}) %all-reduce.11.cloned.1.call-update) | async-done | bytes 131088 | tf_op jit(solution)/shard_map/psum | solution.py:31
  192.6 4.4 %gather_fusion.10 = bf16[1024,256]{1,0:T(8,128)(2,1)S(1)} fusion(bf16[256,256]{1,0:T(8,128)(2,1)} %all-reduce.11.cloned.1.call-done, s32[1024]{0:T(1024)S(1)} %copy-done.7), kind=kCustom, calls=%fused_computation.9.clone | custom fusion | bytes 1052672 | tf_op jit(solution)/shard_map/jit(_take)/gather | solution.py:100
  197.3 0.6 copy-done.1
  198.3 1.0 copy.38
  (131 shorter events, 17.5 us)
Async XLA Ops:
  6.5 77.2 %all-reduce.5.cloned.1.call-start = ((), (), s32[]{:S(2)}) async-start(), calls=%async_computation | async-start | bytes 524288 | tf_op jit(solution)/shard_map/psum | solution.py:87
  6.5 72.4 %collective-permute-start = (bf16[32,1024]{1,0:T(8,128)(2,1)}, bf16[32,1024]{1,0:T(8,128)(2,1)S(1)}, u32[]{:S(2)}, u32[]{:S(2)}) collective-permute-start(bf16[32,1024]{1,0:T(8,128)(2,1)} %param.13), channel_id=1, source_target_pairs={{0,1},{1,2},{2,3},{3,4},{4,5},{5,6},{6,7},{7,0},{8,9},{9,10},{10,1... | collective-permute-start | bytes 196616 | tf_op jit(solution)/shard_map/ppermute | solution.py:20
  9.5 69.5 %collective-permute-start.4 = (bf16[32,1024]{1,0:T(8,128)(2,1)}, bf16[32,1024]{1,0:T(8,128)(2,1)S(1)}, u32[]{:S(2)}, u32[]{:S(2)}) collective-permute-start(bf16[32,1024]{1,0:T(8,128)(2,1)} %param.13), channel_id=1, source_target_pairs={{1,0},{2,1},{3,2},{4,3},{5,4},{6,5},{7,6},{0,7},{9,8},{10,9},{11,1... | collective-permute-start | bytes 196616 | tf_op jit(solution)/shard_map/ppermute | solution.py:22
  12.5 6.0 %copy-start.13 = (pred[256]{0:T(512)(128)(4,1)}, pred[256]{0:T(512)(128)(4,1)S(1)}, u32[]{:S(2)}) copy-start(pred[256]{0:T(512)(128)(4,1)S(1)} %broadcast_compare_fusion.2) | copy-start | bytes 772
  12.5 0.7 copy-start.10
  14.7 1.6 copy-start.2
  16.2 1.2 copy-start.9
  19.5 0.8 copy-start.3
  19.5 95.4 %all-reduce.7.cloned.1.call-start = ((), (), s32[]{:S(2)}) async-start(), calls=%async_computation.1 | async-start | bytes 262144 | tf_op jit(solution)/shard_map/psum | solution.py:31
  20.3 31.9 %copy-start.5 = (s32[256]{0:T(256)}, s32[256]{0:T(256)S(1)}, u32[]{:S(2)}) copy-start(s32[256]{0:T(256)S(1)} %iota_add_fusion.2) | copy-start | bytes 3076
  59.8 0.7 copy-start.11
  79.0 12.3 %collective-permute-start.1 = (bf16[32,1024]{1,0:T(8,128)(2,1)S(1)}, bf16[32,1024]{1,0:T(8,128)(2,1)}, u32[]{:S(2)}, u32[]{:S(2)}) collective-permute-start(bf16[32,1024]{1,0:T(8,128)(2,1)S(1)} %collective-permute-done), channel_id=1, source_target_pairs={{0,1},{1,2},{2,3},{3,4},{4,5},{5,6},{6,7},{7,0},{8,9},{9,10},{10,1... | collective-permute-start | bytes 196616 | tf_op jit(solution)/shard_map/ppermute | solution.py:20
  79.0 12.4 %collective-permute-start.5 = (bf16[32,1024]{1,0:T(8,128)(2,1)S(1)}, bf16[32,1024]{1,0:T(8,128)(2,1)}, u32[]{:S(2)}, u32[]{:S(2)}) collective-permute-start(bf16[32,1024]{1,0:T(8,128)(2,1)S(1)} %collective-permute-done.4), channel_id=1, source_target_pairs={{1,0},{2,1},{3,2},{4,3},{5,4},{6,5},{7,6},{0,7},{9,8},{10,9},{11,1... | collective-permute-start | bytes 196616 | tf_op jit(solution)/shard_map/ppermute | solution.py:22
  85.6 73.3 %all-reduce.9.cloned.1.call-start = ((), (), s32[]{:S(2)}) async-start(), calls=%async_computation.2 | async-start | bytes 524288 | tf_op jit(solution)/shard_map/psum | solution.py:87
  86.2 0.9 slice-start
  91.3 34.1 %collective-permute-start.2 = (bf16[32,1024]{1,0:T(8,128)(2,1)}, bf16[32,1024]{1,0:T(8,128)(2,1)S(1)}, u32[]{:S(2)}, u32[]{:S(2)}) collective-permute-start(bf16[32,1024]{1,0:T(8,128)(2,1)} %collective-permute-done.1), channel_id=1, source_target_pairs={{0,1},{1,2},{2,3},{3,4},{4,5},{5,6},{6,7},{7,0},{8,9},{9,10},{10,1... | collective-permute-start | bytes 196616 | tf_op jit(solution)/shard_map/ppermute | solution.py:20
  91.3 43.7 %collective-permute-start.6 = (bf16[32,1024]{1,0:T(8,128)(2,1)}, bf16[32,1024]{1,0:T(8,128)(2,1)S(1)}, u32[]{:S(2)}, u32[]{:S(2)}) collective-permute-start(bf16[32,1024]{1,0:T(8,128)(2,1)} %collective-permute-done.5), channel_id=1, source_target_pairs={{1,0},{2,1},{3,2},{4,3},{5,4},{6,5},{7,6},{0,7},{9,8},{10,9},{11,1... | collective-permute-start | bytes 196616 | tf_op jit(solution)/shard_map/ppermute | solution.py:22
  119.3 0.9 copy-start
  119.3 0.9 copy-start.19
  119.3 0.9 copy-start.22
  119.3 0.9 copy-start.23
  119.5 0.7 copy-start.18
  124.0 0.6 copy-start.12
  124.0 0.6 copy-start.15
  124.6 0.7 copy-start.14
  125.4 7.0 %collective-permute-start.3 = (bf16[32,1024]{1,0:T(8,128)(2,1)S(1)}, bf16[32,1024]{1,0:T(8,128)(2,1)S(1)}, u32[]{:S(2)}, u32[]{:S(2)}) collective-permute-start(bf16[32,1024]{1,0:T(8,128)(2,1)S(1)} %collective-permute-done.2), channel_id=1, source_target_pairs={{0,1},{1,2},{2,3},{3,4},{4,5},{5,6},{6,7},{7,0},{8,9},{9,10},{10,1... | collective-permute-start | bytes 196616 | tf_op jit(solution)/shard_map/ppermute | solution.py:20
  127.7 64.9 %all-reduce.11.cloned.1.call-start = ((), (), s32[]{:S(2)}) async-start(), calls=%async_computation.3 | async-start | bytes 262144 | tf_op jit(solution)/shard_map/psum | solution.py:31
  133.3 0.8 copy-start.4
  135.8 0.7 copy-start.6
  158.9 1.9 copy-start.8
  160.8 0.9 slice-start.1
  165.6 27.0 %copy-start.7 = (s32[1024]{0:T(1024)S(1)}, s32[1024]{0:T(1024)}, u32[]{:S(2)}) copy-start(s32[1024]{0:T(1024)} %get-tuple-element.20) | copy-start | bytes 12292
  197.0 0.9 copy-start.1
  197.0 0.9 copy-start.17
  197.0 0.9 copy-start.20
  197.0 0.9 copy-start.21
  197.3 0.7 copy-start.16
Sparse Core Ops, SparseCore 0:
  19.6 30.7 all-reduce.4
  85.7 29.1 all-reduce.6
  127.8 31.0 all-reduce.8
  161.2 31.3 all-reduce.10
